TPU v7x, 1024 devices: a whole 4x4x32 slice. The times are simulated.
1024 devices in a mesh: grp: 32 (over z), bal: 32 (over x, y, core).
Axes of the slice: x: 4, y: 4, z: 32, core: 2. Of those that a mesh axis runs over, the one named last changes fastest.
Arguments:
- own_rows: bfloat16 [8192, 32, 512], P(('grp', 'bal')), may hold values from -24 to 24
- work_cotangent: bfloat16 [4096, 32, 512], P(('grp', 'bal')), may hold values from -24 to 24
- seq_lengths: int32 [8192], P('grp'), may hold values from 0 to 32, as said below
- seq_member: int32 [8192], P('grp'), may hold values from -1 to 31, as said below
- w_uvqk: bfloat16 [512, 2048], replicated, may hold values from -0.25 to 0.25
- w_out: bfloat16 [512, 512], replicated, may hold values from -0.25 to 0.25
Outputs:
- member_out: bfloat16 [4096, 32, 512], P(('grp', 'bal'))
- owner_grad: bfloat16 [8192, 32, 512], P(('grp', 'bal'))
- grad_uvqk: float32 [512, 2048], P('bal')
- grad_out: float32 [512, 512], P('bal')
Inputs may be any that keep to these rules, and one draw needn't show every extreme that they name: Slots with seq_member -1 are empty. Every member of a group receives exactly 4 sequences; no owner device sends two sequences to the same member; some owner device holds 8 sequences. `seq_lengths`: 0 exactly on empty slots, 1 or more on the others; each group has a sequence of exactly 32 tokens.
All inputs are finite; a program needn't handle non-finite values.
Results may differ from a plain program's by a relative error of at most 0.028.
Values may be sent and summed in bfloat16 or wider, within the bound.
No kernel may reach another device: no remote copies, remote signals or barrier semaphores. Data moves between devices by JAX's collectives and lax.ppermute only.
A program may use at most 32 MiB of HBM per device.

v0:
```python
import jax
import jax.numpy as jnp
from jax import lax
from jax.sharding import PartitionSpec as P

HEADS = 8


EPSILON = 1e-05


def norm_rows(values):
    centred = values - jnp.mean(values, axis=-1, keepdims=True)
    spread = jnp.mean(centred * centred, axis=-1, keepdims=True)
    return centred * lax.rsqrt(spread + EPSILON)


def silu_slope(values):
    sigma = jax.nn.sigmoid(values)
    return sigma * (1.0 + values * (1.0 - sigma))


def mix_rows(activated, lengths, head_count):
    seq_count, seq_span, proj_width = activated.shape
    model_width = proj_width // 4
    head_size = model_width // head_count
    pieces = activated.reshape(seq_count, seq_span, 4, head_count, head_size)
    gate_part = pieces[:, :, 0].reshape(seq_count, seq_span, model_width).astype(jnp.float32)
    scores = jnp.einsum(
        "sihe,sjhe->shij", pieces[:, :, 2], pieces[:, :, 3], preferred_element_type=jnp.float32
    )
    scores = scores * head_size ** (-0.5)
    position = jnp.arange(seq_span)
    causal = (position[None, :] <= position[:, None]).astype(jnp.float32)
    weights = jax.nn.silu(scores) * causal / lengths.astype(jnp.float32)[:, None, None, None]
    weights = weights.astype(jnp.bfloat16)
    attended = jnp.einsum(
        "shij,sjhe->sihe", weights, pieces[:, :, 1], preferred_element_type=jnp.float32
    )
    return norm_rows(attended.reshape(seq_count, seq_span, model_width)) * gate_part


def layer_rows(rows_x, rows_grad, lengths, w_uvqk, w_out):
    seq_count, seq_span, model_width = rows_x.shape
    total_rows = seq_count * seq_span
    live_mask = (jnp.arange(seq_span)[None, :] < lengths[:, None]).astype(jnp.float32)[:, :, None]
    rows_float = rows_x.astype(jnp.float32)
    normed = norm_rows(rows_float).astype(jnp.bfloat16).reshape(total_rows, model_width)
    projected = jnp.dot(normed, w_uvqk, preferred_element_type=jnp.float32)
    activated = jax.nn.silu(projected).astype(jnp.bfloat16)

    def mixer(values):
        return mix_rows(values.reshape(seq_count, seq_span, -1), lengths, HEADS)

    mixed, mixer_back = jax.vjp(mixer, activated)
    mixed_flat = mixed.astype(jnp.bfloat16).reshape(total_rows, model_width)
    result = jnp.dot(mixed_flat, w_out, preferred_element_type=jnp.float32).reshape(
        seq_count, seq_span, model_width
    )
    result = ((result + rows_float) * live_mask).astype(jnp.bfloat16)
    grad_live = (rows_grad * live_mask).astype(jnp.bfloat16)
    grad_flat = grad_live.reshape(total_rows, model_width)
    grad_mixed = lax.dot_general(
        grad_flat, w_out, (((1,), (1,)), ((), ())), preferred_element_type=jnp.float32
    )
    grad_act = mixer_back(grad_mixed.reshape(seq_count, seq_span, model_width))[0]
    grad_proj = (grad_act.astype(jnp.float32) * silu_slope(projected)).astype(jnp.bfloat16)
    grad_normed = lax.dot_general(
        grad_proj, w_uvqk, (((1,), (1,)), ((), ())), preferred_element_type=jnp.float32
    )
    _, norm_back = jax.vjp(norm_rows, rows_float)
    grad_rows = norm_back(grad_normed.reshape(seq_count, seq_span, model_width))[
        0
    ] + grad_live.astype(jnp.float32)
    grad_rows = (grad_rows * live_mask).astype(jnp.bfloat16)
    return (result, grad_rows, (normed, grad_proj, mixed_flat, grad_flat))


def body(own_rows, work_cotangent, seq_lengths, seq_member, w_uvqk, w_out):
    members = lax.axis_size("bal")
    my_index = lax.axis_index("bal")
    own_count, seq_span, model_width = own_rows.shape
    work_count = work_cotangent.shape[0]
    pair_cap = -(-own_count // members)
    item_count = members * pair_cap
    member_of = seq_member.reshape(members, own_count)
    length_of = seq_lengths.reshape(members, own_count)
    slot_ids = jnp.arange(own_count)
    same_member = (member_of[:, :, None] == member_of[:, None, :]) & (
        slot_ids[None, None, :] < slot_ids[None, :, None]
    )
    pair_rank = jnp.sum(same_member.astype(jnp.int32), axis=2)
    my_members = lax.dynamic_index_in_dim(member_of, my_index, 0, keepdims=False)
    my_ranks = lax.dynamic_index_in_dim(pair_rank, my_index, 0, keepdims=False)
    item_ids = jnp.arange(item_count)
    send_pick = ((my_members * pair_cap + my_ranks)[None, :] == item_ids[:, None]) & (
        my_members >= 0
    )[None, :]
    send_pick = send_pick.astype(jnp.bfloat16)
    outgoing = jnp.dot(
        send_pick,
        own_rows.reshape(own_count, seq_span * model_width),
        preferred_element_type=jnp.float32,
    )
    incoming = lax.all_to_all(
        outgoing.astype(jnp.bfloat16), "bal", split_axis=0, concat_axis=0, tiled=True
    )
    to_me = member_of == my_index
    rank_ids = jnp.arange(pair_cap)
    hit_table = (to_me[:, :, None] & (pair_rank[:, :, None] == rank_ids[None, None, :])).astype(
        jnp.int32
    )
    item_live = jnp.sum(hit_table, axis=1).reshape(item_count)
    item_length = jnp.sum(hit_table * length_of[:, :, None], axis=1).reshape(item_count)
    position = jnp.cumsum(item_live) - 1
    work_ids = jnp.arange(work_count)
    pick_work = (item_live[None, :] > 0) & (position[None, :] == work_ids[:, None])
    work_rows = jnp.dot(
        pick_work.astype(jnp.bfloat16), incoming, preferred_element_type=jnp.float32
    )
    work_rows = work_rows.astype(jnp.bfloat16).reshape(work_count, seq_span, model_width)
    work_lengths = jnp.sum(pick_work.astype(jnp.int32) * item_length[None, :], axis=1)
    result, grad_rows, factors = layer_rows(work_rows, work_cotangent, work_lengths, w_uvqk, w_out)
    normed, grad_proj, mixed_flat, grad_flat = factors
    back_items = lax.dot_general(
        pick_work.astype(jnp.bfloat16),
        grad_rows.reshape(work_count, seq_span * model_width),
        (((0,), (0,)), ((), ())),
        preferred_element_type=jnp.float32,
    )
    returned = lax.all_to_all(
        back_items.astype(jnp.bfloat16), "bal", split_axis=0, concat_axis=0, tiled=True
    )
    own_grad = lax.dot_general(
        send_pick, returned, (((0,), (0,)), ((), ())), preferred_element_type=jnp.float32
    )
    own_grad = own_grad.astype(jnp.bfloat16).reshape(own_count, seq_span, model_width)
    term_uvqk = lax.dot_general(
        normed, grad_proj, (((0,), (0,)), ((), ())), preferred_element_type=jnp.float32
    )
    term_out = lax.dot_general(
        mixed_flat, grad_flat, (((0,), (0,)), ((), ())), preferred_element_type=jnp.float32
    )
    part_uvqk, part_out = (
        lax.psum_scatter(
            term_uvqk.astype(jnp.bfloat16), "bal", scatter_dimension=0, tiled=True
        ).astype(jnp.float32),
        lax.psum_scatter(
            term_out.astype(jnp.bfloat16), "bal", scatter_dimension=0, tiled=True
        ).astype(jnp.float32),
    )
    grad_uvqk, grad_out = (
        lax.psum(part_uvqk.astype(jnp.bfloat16), "grp").astype(jnp.float32),
        lax.psum(part_out.astype(jnp.bfloat16), "grp").astype(jnp.float32),
    )
    return (result, own_grad, grad_uvqk, grad_out)


def solution(mesh):
    placed = (
        P(("grp", "bal"), None, None),
        P(("grp", "bal"), None, None),
        P("grp"),
        P("grp"),
        P(),
        P(),
    )
    return jax.shard_map(
        body,
        mesh=mesh,
        in_specs=placed,
        out_specs=(
            P(("grp", "bal"), None, None),
            P(("grp", "bal"), None, None),
            P("bal", None),
            P("bal", None),
        ),
        check_vma=False,
    )
```

profile of v0, /device:TPU:2, one launch (start us, length us, event | category | flops | bytes accessed | tf_op | source)
XLA Modules:
  0.0 609.5 jit_solution(17434342836645104341)
XLA Ops:
  10.7 2.1 reduce.12
  12.8 2.7 reshape.311
  15.5 16.8 %all-to-all-start = ((bf16[32,2,8192]{2,1,0:T(2,128)(2,1)}), bf16[32,2,8192]{2,1,0:T(2,128)(2,1)S(1)}, u32[]{:S(2)}, u32[]{:S(2)}) async-start(bf16[32,2,8192]{2,1,0:T(2,128)(2,1)} %reshape.311), calls=%async_computation | async-start | bytes 2097152 | tf_op jit(solution)/shard_map/all_to_all | solution.py:105
  33.3 13.5 %all-to-all-done = bf16[32,2,8192]{2,1,0:T(2,128)(2,1)S(1)} async-done(((bf16[32,2,8192]{2,1,0:T(2,128)(2,1)}), bf16[32,2,8192]{2,1,0:T(2,128)(2,1)S(1)}, u32[]{:S(2)}, u32[]{:S(2)}) %all-to-all-start) | async-done | bytes 1048608 | tf_op jit(solution)/shard_map/all_to_all | solution.py:105
  46.8 3.5 reshape.312
  50.3 2.8 fusion.2
  53.8 1.7 multiply_convert_fusion.1
  55.5 2.1 reshape.295
  67.0 1.4 fusion.18
  69.6 2.6 copy.90
  72.2 2.9 reshape.305
  76.5 1.9 multiply_convert_fusion
  78.4 2.2 convolution_convert_fusion.4
  85.9 2.1 reduce.13
  88.0 2.7 reshape.313
  90.6 6.4 %all-to-all-start.1 = ((bf16[32,2,8192]{2,1,0:T(2,128)(2,1)}), bf16[32,2,8192]{2,1,0:T(2,128)(2,1)S(1)}, u32[]{:S(2)}, u32[]{:S(2)}) async-start(bf16[32,2,8192]{2,1,0:T(2,128)(2,1)} %reshape.313), calls=%async_computation.1 | async-start | bytes 2097152 | tf_op jit(solution)/shard_map/all_to_all | solution.py:131
  97.1 1.9 fusion.11
  99.0 105.8 %reduce-scatter.5.cloned.1.call-done = bf16[16,512]{1,0:T(8,128)(2,1)} async-done(((bf16[512,512]{1,0:T(8,128)(2,1)}), bf16[16,512]{1,0:T(8,128)(2,1)}) %reduce-scatter.5.cloned.1.call-update) | async-done | bytes 16400 | tf_op jit(solution)/shard_map/reduce_scatter | solution.py:148
  204.8 109.9 %psum.15 = bf16[16,512]{1,0:T(8,128)(2,1)S(1)} all-reduce(bf16[16,512]{1,0:T(8,128)(2,1)} %reduce-scatter.5.cloned.1.call-done), channel_id=1, replica_groups=mesh['grp'=32,'bal'=32] {'grp'}, use_global_device_ids=true, to_apply=%region_16.17 | all-reduce | flops 8192 | bytes 32768 | tf_op jit(solution)/shard_map/psum | solution.py:154
  315.4 3.5 reshape.314
  318.9 24.1 %reduce-scatter.3.cloned.1.call-done = bf16[16,2048]{1,0:T(8,128)(2,1)} async-done(((bf16[512,2048]{1,0:T(8,128)(2,1)}), bf16[16,2048]{1,0:T(8,128)(2,1)}) %reduce-scatter.3.cloned.1.call-update) | async-done | bytes 65552 | tf_op jit(solution)/shard_map/reduce_scatter | solution.py:145
  343.1 2.8 convolution_convert_fusion.2
  346.7 254.8 %all-reduce.6.cloned.1.call-done = bf16[16,2048]{1,0:T(8,128)(2,1)} async-done(((bf16[16,2048]{1,0:T(8,128)(2,1)}), bf16[16,2048]{1,0:T(8,128)(2,1)}) %all-reduce.6.cloned.1.call-update) | async-done | bytes 65552 | tf_op jit(solution)/shard_map/psum | solution.py:153
  601.5 1.5 convert_element_type.194
  (133 shorter events, 23.6 us)
Async XLA Ops:
  7.2 46.6 %copy-start = (bf16[512,2048]{1,0:T(8,128)(2,1)S(1)}, bf16[512,2048]{1,0:T(8,128)(2,1)}, u32[]{:S(2)}) copy-start(bf16[512,2048]{1,0:T(8,128)(2,1)} %param.10) | copy-start | bytes 6291460
  8.5 7.0 %copy-start.20 = (pred[8]{0:T(512)(128)(4,1)}, pred[8]{0:T(512)(128)(4,1)S(1)}, u32[]{:S(2)}) copy-start(pred[8]{0:T(512)(128)(4,1)S(1)} %compare_reduce_fusion) | copy-start | bytes 28
  8.7 6.8 %copy-start.22 = (s32[8]{0:T(128)}, s32[8]{0:T(128)S(1)}, u32[]{:S(2)}) copy-start(s32[8]{0:T(128)S(1)} %add_reduce_fusion.1) | copy-start | bytes 100
  12.8 19.5 %copy-start.25 = (s32[256]{0:T(256)S(1)}, s32[256]{0:T(256)}, u32[]{:S(2)}) copy-start(s32[256]{0:T(256)} %param.9) | copy-start | bytes 3076
  12.8 19.7 %copy-start.28 = (s32[256]{0:T(256)S(1)}, s32[256]{0:T(256)}, u32[]{:S(2)}) copy-start(s32[256]{0:T(256)} %param.8) | copy-start | bytes 3076
  15.5 31.3 %all-to-all-start = ((bf16[32,2,8192]{2,1,0:T(2,128)(2,1)}), bf16[32,2,8192]{2,1,0:T(2,128)(2,1)S(1)}, u32[]{:S(2)}, u32[]{:S(2)}) async-start(bf16[32,2,8192]{2,1,0:T(2,128)(2,1)} %reshape.311), calls=%async_computation | async-start | bytes 2097152 | tf_op jit(solution)/shard_map/all_to_all | solution.py:105
  32.3 172.5 %reduce-scatter.5.cloned.1.call-start = ((), (), s32[]{:S(2)}) async-start(), calls=%async_computation.6 | async-start | bytes 540672 | tf_op jit(solution)/shard_map/reduce_scatter | solution.py:148
  33.0 20.0 %copy-start.17 = (s32[32]{0:T(128)}, s32[32]{0:T(128)S(1)}, u32[]{:S(2)}) copy-start(s32[32]{0:T(128)S(1)} %add_reduce_fusion) | copy-start | bytes 388
  33.0 20.0 %copy-start.24 = (pred[32]{0:T(512)(128)(4,1)}, pred[32]{0:T(512)(128)(4,1)S(1)}, u32[]{:S(2)}) copy-start(pred[32]{0:T(512)(128)(4,1)S(1)} %broadcast_compare_fusion.1) | copy-start | bytes 100
  33.2 25.4 %copy-start.30 = (f32[4]{0:T(128)}, f32[4]{0:T(128)S(1)}, u32[]{:S(2)}) copy-start(f32[4]{0:T(128)S(1)} %convert_element_type.168) | copy-start | bytes 52
  33.2 25.4 %copy-start.16 = (f32[32,32]{1,0:T(8,128)}, f32[32,32]{1,0:T(8,128)S(1)}, u32[]{:S(2)}) copy-start(f32[32,32]{1,0:T(8,128)S(1)} %fusion.37) | copy-start | bytes 12292
  59.7 4.7 copy-start.3
  59.7 4.7 copy-start.12
  72.2 2.9 copy-start.13
  72.2 2.9 copy-start.14
  75.1 3.3 copy-start.2
  75.1 3.3 copy-start.19
  75.1 3.3 copy-start.27
  76.3 266.8 %reduce-scatter.3.cloned.1.call-start = ((), (), s32[]{:S(2)}) async-start(), calls=%async_computation.4 | async-start | bytes 2162688 | tf_op jit(solution)/shard_map/reduce_scatter | solution.py:145
  88.0 9.1 %copy-start.15 = (bf16[4,32,512]{2,1,0:T(8,128)(2,1)S(1)}, bf16[4,32,512]{2,1,0:T(8,128)(2,1)}, u32[]{:S(2)}) copy-start(bf16[4,32,512]{2,1,0:T(8,128)(2,1)} %get-tuple-element.37) | copy-start | bytes 393220
  90.6 224.8 %all-to-all-start.1 = ((bf16[32,2,8192]{2,1,0:T(2,128)(2,1)}), bf16[32,2,8192]{2,1,0:T(2,128)(2,1)S(1)}, u32[]{:S(2)}, u32[]{:S(2)}) async-start(bf16[32,2,8192]{2,1,0:T(2,128)(2,1)} %reshape.313), calls=%async_computation.1 | async-start | bytes 2097152 | tf_op jit(solution)/shard_map/all_to_all | solution.py:131
  97.0 246.0 %copy-start.21 = (pred[8]{0:T(512)(128)(4,1)S(1)}, pred[8]{0:T(512)(128)(4,1)}, u32[]{:S(2)}) copy-start(pred[8]{0:T(512)(128)(4,1)} %copy-done.20) | copy-start | bytes 28
  97.0 246.0 %copy-start.23 = (s32[8]{0:T(128)S(1)}, s32[8]{0:T(128)}, u32[]{:S(2)}) copy-start(s32[8]{0:T(128)} %copy-done.22) | copy-start | bytes 100
  97.0 504.4 %all-reduce.6.cloned.1.call-start = ((), (), s32[]{:S(2)}) async-start(), calls=%async_computation.5 | async-start | bytes 131072 | tf_op jit(solution)/shard_map/psum | solution.py:153
  (12 other events, 19.3 us)
Sparse Core Ops, SparseCore 0:
  76.4 128.4 reduce-scatter.4
  210.4 132.5 reduce-scatter.2
  345.4 256.0 all-reduce.5
where the time goes:
time: 610 us; the launch traced here: 609 us
  waiting for transfers between devices  398 us (65%)
  blocking collectives  110 us (18%)
  local copies, waits for them, and re-layouts  28.9 us (5%)
  starting transfers between devices  23.5 us (4%)
  matrix products  19.5 us (3%)
  other arithmetic  15.1 us (2%)
  between operations  14.3 us (2%)
    psum x1, waiting for transfers between devices, body(): lax.psum(part_uvqk.astype(jnp.bfloat16), 'grp').astype(jnp.float32)  255 us
    psum x1, blocking collectives, body(): lax.psum(part_out.astype(jnp.bfloat16), 'grp').astype(jnp.float32)  110 us
    reduce_scatter x1, waiting for transfers between devices, body(): lax.psum_scatter(term_out.astype(jnp.bfloat16), 'bal', scatter_dimension=...  106 us
    reduce_scatter x1, waiting for transfers between devices, body(): lax.psum_scatter(term_uvqk.astype(jnp.bfloat16), 'bal', scatter_dimension...  24.1 us
    all_to_all x1, starting transfers between devices, body(): lax.all_to_all(outgoing.astype(jnp.bfloat16), 'bal', split_axis=0, concat...  16.8 us
    unnamed x69, local copies, waits for them, and re-layouts  14.4 us
    all_to_all x1, waiting for transfers between devices, body(): lax.all_to_all(outgoing.astype(jnp.bfloat16), 'bal', split_axis=0, concat...  13.5 us
  transfers between devices with their start and end apart: 5, of which 4 were waited for; matrix products, arithmetic and copies ran while one was open for 4% of the time, Pallas kernels for 0%

commit v1 on v0

--- a/solution.py
+++ b/solution.py
@@ -76,6 +76,35 @@
     return (result, grad_rows, (normed, grad_proj, mixed_flat, grad_flat))
 
 
+def swap_pieces(pieces, axis, groups=None):
+    return lax.all_to_all(
+        pieces, axis, split_axis=0, concat_axis=0, tiled=True, axis_index_groups=groups
+    )
+
+
+def reduce_terms(terms, model_width):
+    members = lax.axis_size("bal")
+    groups = lax.axis_size("grp")
+    chips = members // 2
+    rows, width = terms.shape
+    part_rows = rows // members
+    core_pairs = [[2 * chip, 2 * chip + 1] for chip in range(chips)]
+    same_core = [[2 * chip + core for chip in range(chips)] for core in range(2)]
+    by_core = terms.reshape(chips, 2, part_rows, width).transpose(1, 0, 2, 3)
+    halves = swap_pieces(by_core.reshape(2, chips * part_rows, width), "bal", core_pairs)
+    chip_sum = jnp.sum(halves.astype(jnp.float32), axis=0).astype(jnp.bfloat16)
+    slices = swap_pieces(chip_sum.reshape(chips, part_rows, width), "bal", same_core)
+    part = jnp.sum(slices.astype(jnp.float32), axis=0).astype(jnp.bfloat16)
+    pair_rows, cuts = 2, groups * 2 // part_rows
+    pieces = part.reshape(part_rows // pair_rows, pair_rows, cuts, width // cuts)
+    pieces = pieces.transpose(0, 2, 1, 3).reshape(groups, pair_rows, width // cuts)
+    piece = jnp.sum(swap_pieces(pieces, "grp").astype(jnp.float32), axis=0).astype(jnp.bfloat16)
+    spread = swap_pieces(jnp.broadcast_to(piece[None], pieces.shape), "grp")
+    total = spread.reshape(part_rows // pair_rows, cuts, pair_rows, width // cuts)
+    total = total.transpose(0, 2, 1, 3).reshape(part_rows, width).astype(jnp.float32)
+    return total[:, : width - model_width], total[:, width - model_width :]
+
+
 def body(own_rows, work_cotangent, seq_lengths, seq_member, w_uvqk, w_out):
     members = lax.axis_size("bal")
     my_index = lax.axis_index("bal")
@@ -141,18 +170,8 @@
     term_out = lax.dot_general(
         mixed_flat, grad_flat, (((0,), (0,)), ((), ())), preferred_element_type=jnp.float32
     )
-    part_uvqk, part_out = (
-        lax.psum_scatter(
-            term_uvqk.astype(jnp.bfloat16), "bal", scatter_dimension=0, tiled=True
-        ).astype(jnp.float32),
-        lax.psum_scatter(
-            term_out.astype(jnp.bfloat16), "bal", scatter_dimension=0, tiled=True
-        ).astype(jnp.float32),
-    )
-    grad_uvqk, grad_out = (
-        lax.psum(part_uvqk.astype(jnp.bfloat16), "grp").astype(jnp.float32),
-        lax.psum(part_out.astype(jnp.bfloat16), "grp").astype(jnp.float32),
-    )
+    terms = jnp.concatenate([term_uvqk, term_out], axis=1).astype(jnp.bfloat16)
+    grad_uvqk, grad_out = reduce_terms(terms, model_width)
     return (result, own_grad, grad_uvqk, grad_out)
 
 

time: 610 us -> 226 us (0.37)
  the two profiles are of different devices: /device:TPU:2 before, /device:TPU:1 now
where the time goes in v1:
time: 226 us; the launch traced here: 225 us
  waiting for transfers between devices  67.8 us (30%)
  starting transfers between devices  49.2 us (22%)
  local copies, waits for them, and re-layouts  35.2 us (16%)
  blocking collectives  30.1 us (13%)
  other arithmetic  21.1 us (9%)
  matrix products  20.3 us (9%)
    all_to_all x2, waiting for transfers between devices, swap_pieces(): lax.all_to_all(pieces, axis, split_axis=0, concat_axis=0, tiled=True, axi...  35.8 us
    all_to_all x2, blocking collectives, swap_pieces(): lax.all_to_all(pieces, axis, split_axis=0, concat_axis=0, tiled=True, axi...  30.1 us
    all_to_all x2, starting transfers between devices, swap_pieces(): lax.all_to_all(pieces, axis, split_axis=0, concat_axis=0, tiled=True, axi...  23.9 us
    all_to_all x1, starting transfers between devices, body(): lax.all_to_all(outgoing.astype(jnp.bfloat16), 'bal', split_axis=0, concat...  17.7 us
    all_to_all x1, waiting for transfers between devices, body(): lax.all_to_all(outgoing.astype(jnp.bfloat16), 'bal', split_axis=0, concat...  16.1 us
    all_to_all x1, waiting for transfers between devices, body(): lax.all_to_all(back_items.astype(jnp.bfloat16), 'bal', split_axis=0, conc...  15.9 us
    unnamed x72, local copies, waits for them, and re-layouts  14.8 us
    all_to_all x1, starting transfers between devices, body(): lax.all_to_all(back_items.astype(jnp.bfloat16), 'bal', split_axis=0, conc...  7.54 us
  transfers between devices with their start and end apart: 4, of which 4 were waited for; matrix products, arithmetic and copies ran while one was open for 8% of the time, Pallas kernels for 0%

profile of v1, /device:TPU:1, one launch (start us, length us, event | category | flops | bytes accessed | tf_op | source)
XLA Modules:
  0.0 224.9 jit_solution(17963624297815977362)
XLA Ops:
  4.2 2.1 reduce.15
  6.3 2.7 %reshape.343 = bf16[32,2,8192]{2,1,0:T(2,128)(2,1)} reshape(bf16[32,16384]{1,0:T(8,128)(2,1)} %reduce.15) | data formatting | bytes 2097152
  9.0 17.7 %all-to-all-start = ((bf16[32,2,8192]{2,1,0:T(2,128)(2,1)}), bf16[32,2,8192]{2,1,0:T(2,128)(2,1)S(1)}, u32[]{:S(2)}, u32[]{:S(2)}) async-start(bf16[32,2,8192]{2,1,0:T(2,128)(2,1)} %reshape.343), calls=%async_computation | async-start | bytes 2097152 | tf_op jit(solution)/shard_map/all_to_all | solution.py:134
  27.6 16.1 %all-to-all-done = bf16[32,2,8192]{2,1,0:T(2,128)(2,1)S(1)} async-done(((bf16[32,2,8192]{2,1,0:T(2,128)(2,1)}), bf16[32,2,8192]{2,1,0:T(2,128)(2,1)S(1)}, u32[]{:S(2)}, u32[]{:S(2)}) %all-to-all-start) | async-done | bytes 1048608 | tf_op jit(solution)/shard_map/all_to_all | solution.py:134
  43.7 3.5 %reshape.344 = bf16[32,1,16384]{2,1,0:T(2,128)(2,1)} reshape(bf16[32,2,8192]{2,1,0:T(2,128)(2,1)S(1)} %all-to-all-done) | data formatting | bytes 2097152
  47.1 2.8 %fusion.2 = f32[4,16384]{1,0:T(4,128)S(1)} fusion(bf16[32,1,16384]{2,1,0:T(2,128)(2,1)} %reshape.344, s32[32]{0:T(128)S(1)} %add_reduce_fusion, pred[32]{0:T(512)(128)(4,1)S(1)} %broadcast_compare_fusion.1), kind=kOutput, calls=%fused_computation.6 | convolution fusion | flops 4325632 | bytes 1310880 | tf_op jit(solution)/shard_map/dot_general | solution.py:147
  52.4 2.1 reshape.319
  70.0 2.6 %copy.131 = f32[4,32,4,8,64]{4,3,2,1,0:T(8,128)} copy(f32[4,32,4,8,64]{4,1,3,0,2:T(8,128)S(1)} %add_convert_fusion) | data formatting | bytes 2097152 | tf_op jit(solution)/shard_map/convert_element_type | solution.py:67
  72.5 2.8 %reshape.333 = f32[128,2048]{1,0:T(8,128)} reshape(f32[4,32,4,8,64]{4,3,2,1,0:T(8,128)} %copy.131) | data formatting | bytes 2097152 | tf_op jit(solution)/shard_map/convert_element_type | solution.py:67
  75.4 1.9 multiply_convert_fusion
  80.3 2.9 %convolution_convert_fusion.4 = bf16[16,2,16,2048]{3,2,1,0:T(8,128)(2,1)} fusion(bf16[16,2,16,128]{3,2,1,0:T(8,128)(2,1)} %bitcast.139, bf16[128,2048]{1,0:T(8,128)(2,1)S(1)} %multiply_convert_fusion), kind=kOutput, calls=%fused_computation.7 | convolution fusion | flops 269484032 | bytes 2752512 | tf_op jit(solution)/shard_map/dot_general | solution.py:167
  86.3 6.5 %all_to_all.44 = bf16[2,256,2560]{2,1,0:T(8,128)(2,1)} all-to-all(bf16[2,256,2560]{2,1,0:T(8,128)(2,1)S(1)} %bitcast.124), channel_id=1, replica_groups={{0,1},{2,3},{4,5},{6,7},{8,9},{10,11},{12,13},{14,15},{16,17},{18,19},{..., dimensions={0} | all-to-all | bytes 5242880 | tf_op jit(solution)/shard_map/all_to_all | solution.py:80
  92.8 3.6 %reduce_sum.183 = bf16[256,2560]{1,0:T(8,128)(2,1)} reduce(bf16[2,256,2560]{2,1,0:T(8,128)(2,1)} %all_to_all.44, bf16[]{:T(256)} %constant.52.clone.1), dimensions={0}, to_apply=%region_13.14 | reduce | flops 655360 | bytes 3932162 | tf_op jit(solution)/shard_map/reduce_sum | solution.py:95
  96.4 23.6 %all_to_all.45 = bf16[16,16,2560]{2,1,0:T(8,128)(2,1)} all-to-all(bf16[16,16,2560]{2,1,0:T(8,128)(2,1)} %bitcast.129), channel_id=1, replica_groups={{0,2,4,6,8,10,12,14,16,18,20,22,24,26,28,30},{1,3,5,7,9,11,13,15,17,19,..., dimensions={0} | all-to-all | bytes 2621440 | tf_op jit(solution)/shard_map/all_to_all | solution.py:80
  122.3 19.3 %all-to-all-start.4 = ((bf16[32,2,640]{2,1,0:T(2,128)(2,1)}), bf16[32,2,640]{2,1,0:T(2,128)(2,1)}, u32[]{:S(2)}, u32[]{:S(2)}) async-start(bf16[32,2,640]{2,1,0:T(2,128)(2,1)} %bitcast.31), calls=%async_computation.4 | async-start | bytes 163840 | tf_op jit(solution)/shard_map/all_to_all | solution.py:80
  143.3 2.1 reduce.16
  145.5 2.6 %reshape.345 = bf16[32,2,8192]{2,1,0:T(2,128)(2,1)} reshape(bf16[32,16384]{1,0:T(8,128)(2,1)} %reduce.16) | data formatting | bytes 2097152
  148.1 18.2 %all-to-all-done.4 = bf16[32,2,640]{2,1,0:T(2,128)(2,1)} async-done(((bf16[32,2,640]{2,1,0:T(2,128)(2,1)}), bf16[32,2,640]{2,1,0:T(2,128)(2,1)}, u32[]{:S(2)}, u32[]{:S(2)}) %all-to-all-start.4) | async-done | bytes 81952 | tf_op jit(solution)/shard_map/all_to_all | solution.py:80
  166.3 7.5 %all-to-all-start.1 = ((bf16[32,2,8192]{2,1,0:T(2,128)(2,1)}), bf16[32,2,8192]{2,1,0:T(2,128)(2,1)S(1)}, u32[]{:S(2)}, u32[]{:S(2)}) async-start(bf16[32,2,8192]{2,1,0:T(2,128)(2,1)} %reshape.345), calls=%async_computation.1 | async-start | bytes 2097152 | tf_op jit(solution)/shard_map/all_to_all | solution.py:160
  174.8 15.9 %all-to-all-done.1 = bf16[32,2,8192]{2,1,0:T(2,128)(2,1)S(1)} async-done(((bf16[32,2,8192]{2,1,0:T(2,128)(2,1)}), bf16[32,2,8192]{2,1,0:T(2,128)(2,1)S(1)}, u32[]{:S(2)}, u32[]{:S(2)}) %all-to-all-start.1) | async-done | bytes 1048608 | tf_op jit(solution)/shard_map/all_to_all | solution.py:160
  191.4 4.6 %all-to-all-start.5 = ((bf16[32,2,640]{2,1,0:T(2,128)(2,1)}), bf16[32,2,640]{2,1,0:T(2,128)(2,1)}, u32[]{:S(2)}, u32[]{:S(2)}) async-start(bf16[32,2,640]{2,1,0:T(2,128)(2,1)} %broadcast_in_dim.26), calls=%async_computation.5 | async-start | bytes 163840 | tf_op jit(solution)/shard_map/all_to_all | solution.py:80
  198.0 3.5 %reshape.346 = bf16[32,1,16384]{2,1,0:T(2,128)(2,1)} reshape(bf16[32,2,8192]{2,1,0:T(2,128)(2,1)S(1)} %all-to-all-done.1) | data formatting | bytes 2097152
  201.4 2.8 %convolution_convert_fusion.2 = bf16[8,16384]{1,0:T(8,128)(2,1)S(1)} fusion(bf16[32,1,16384]{2,1,0:T(2,128)(2,1)} %reshape.346, s32[8]{0:T(128)S(1)} %copy-done.18, pred[8]{0:T(512)(128)(4,1)S(1)} %copy-done.16), kind=kOutput, calls=%fused_computation.4 | convolution fusion | flops 8520192 | bytes 1310760 | tf_op jit(solution)/shard_map/dot_general | solution.py:163
  205.0 17.6 %all-to-all-done.5 = bf16[32,2,640]{2,1,0:T(2,128)(2,1)} async-done(((bf16[32,2,640]{2,1,0:T(2,128)(2,1)}), bf16[32,2,640]{2,1,0:T(2,128)(2,1)}, u32[]{:S(2)}, u32[]{:S(2)}) %all-to-all-start.5) | async-done | bytes 81952 | tf_op jit(solution)/shard_map/all_to_all | solution.py:80
  (144 shorter events, 38.6 us)
Async XLA Ops:
  0.6 50.1 %copy-start = (bf16[512,2048]{1,0:T(8,128)(2,1)S(1)}, bf16[512,2048]{1,0:T(8,128)(2,1)}, u32[]{:S(2)}) copy-start(bf16[512,2048]{1,0:T(8,128)(2,1)} %param.10) | copy-start | bytes 6291460
  6.3 20.4 %copy-start.22 = (s32[256]{0:T(256)S(1)}, s32[256]{0:T(256)}, u32[]{:S(2)}) copy-start(s32[256]{0:T(256)} %param.9) | copy-start | bytes 3076
  6.3 20.6 %copy-start.25 = (s32[256]{0:T(256)S(1)}, s32[256]{0:T(256)}, u32[]{:S(2)}) copy-start(s32[256]{0:T(256)} %param.8) | copy-start | bytes 3076
  9.0 34.7 %all-to-all-start = ((bf16[32,2,8192]{2,1,0:T(2,128)(2,1)}), bf16[32,2,8192]{2,1,0:T(2,128)(2,1)S(1)}, u32[]{:S(2)}, u32[]{:S(2)}) async-start(bf16[32,2,8192]{2,1,0:T(2,128)(2,1)} %reshape.343), calls=%async_computation | async-start | bytes 2097152 | tf_op jit(solution)/shard_map/all_to_all | solution.py:134
  27.4 22.6 %copy-start.14 = (s32[32]{0:T(128)}, s32[32]{0:T(128)S(1)}, u32[]{:S(2)}) copy-start(s32[32]{0:T(128)S(1)} %add_reduce_fusion) | copy-start | bytes 388
  27.4 22.6 %copy-start.21 = (pred[32]{0:T(512)(128)(4,1)}, pred[32]{0:T(512)(128)(4,1)S(1)}, u32[]{:S(2)}) copy-start(pred[32]{0:T(512)(128)(4,1)S(1)} %broadcast_compare_fusion.1) | copy-start | bytes 100
  27.5 28.0 %copy-start.31 = (f32[4]{0:T(128)}, f32[4]{0:T(128)S(1)}, u32[]{:S(2)}) copy-start(f32[4]{0:T(128)S(1)} %convert_element_type.172) | copy-start | bytes 52
  27.5 28.0 %copy-start.13 = (f32[32,32]{1,0:T(8,128)}, f32[32,32]{1,0:T(8,128)S(1)}, u32[]{:S(2)}) copy-start(f32[32,32]{1,0:T(8,128)S(1)} %fusion.39) | copy-start | bytes 12292
  50.4 2.0 copy-start.19
  50.6 1.8 copy-start.1
  56.6 4.7 %copy-start.3 = (bf16[512,512]{1,0:T(8,128)(2,1)S(1)}, bf16[512,512]{1,0:T(8,128)(2,1)}, u32[]{:S(2)}) copy-start(bf16[512,512]{1,0:T(8,128)(2,1)} %param.11) | copy-start | bytes 1572868
  56.6 4.7 %copy-start.11 = (bf16[4,32,512]{2,1,0:T(8,128)(2,1)S(1)}, bf16[4,32,512]{2,1,0:T(8,128)(2,1)}, u32[]{:S(2)}) copy-start(bf16[4,32,512]{2,1,0:T(8,128)(2,1)} %param.7) | copy-start | bytes 393220
  61.7 3.1 %copy-start.9 = (bf16[4,32,1,8,64]{4,3,2,1,0:T(8,128)(2,1)S(1)}, bf16[4,32,1,8,64]{4,3,2,1,0:T(8,128)(2,1)}, u32[]{:S(2)}) copy-start(bf16[4,32,1,8,64]{4,3,2,1,0:T(8,128)(2,1)} %copy-done.8) | copy-start | bytes 393220
  64.8 1.7 copy-start.5
  75.4 2.0 copy-start.2
  75.4 2.0 copy-start.20
  78.8 4.7 %copy-start.12 = (bf16[4,32,512]{2,1,0:T(8,128)(2,1)S(1)}, bf16[4,32,512]{2,1,0:T(8,128)(2,1)}, u32[]{:S(2)}) copy-start(bf16[4,32,512]{2,1,0:T(8,128)(2,1)} %param.7) | copy-start | bytes 393220
  96.4 45.2 %copy-start.28 = (f32[128]{0:T(128)S(1)}, f32[128]{0:T(128)}, u32[]{:S(2)}) copy-start(f32[128]{0:T(128)} %get-tuple-element.43) | copy-start | bytes 1540
  96.4 45.2 %copy-start.24 = (f32[128]{0:T(128)S(1)}, f32[128]{0:T(128)}, u32[]{:S(2)}) copy-start(f32[128]{0:T(128)} %copy-done.23) | copy-start | bytes 1540
  122.3 44.0 %all-to-all-start.4 = ((bf16[32,2,640]{2,1,0:T(2,128)(2,1)}), bf16[32,2,640]{2,1,0:T(2,128)(2,1)}, u32[]{:S(2)}, u32[]{:S(2)}) async-start(bf16[32,2,640]{2,1,0:T(2,128)(2,1)} %bitcast.31), calls=%async_computation.4 | async-start | bytes 163840 | tf_op jit(solution)/shard_map/all_to_all | solution.py:80
  166.3 24.5 %all-to-all-start.1 = ((bf16[32,2,8192]{2,1,0:T(2,128)(2,1)}), bf16[32,2,8192]{2,1,0:T(2,128)(2,1)S(1)}, u32[]{:S(2)}, u32[]{:S(2)}) async-start(bf16[32,2,8192]{2,1,0:T(2,128)(2,1)} %reshape.345), calls=%async_computation.1 | async-start | bytes 2097152 | tf_op jit(solution)/shard_map/all_to_all | solution.py:160
  191.4 31.1 %all-to-all-start.5 = ((bf16[32,2,640]{2,1,0:T(2,128)(2,1)}), bf16[32,2,640]{2,1,0:T(2,128)(2,1)}, u32[]{:S(2)}, u32[]{:S(2)}) async-start(bf16[32,2,640]{2,1,0:T(2,128)(2,1)} %broadcast_in_dim.26), calls=%async_computation.5 | async-start | bytes 163840 | tf_op jit(solution)/shard_map/all_to_all | solution.py:80
  196.0 5.4 %copy-start.16 = (pred[8]{0:T(512)(128)(4,1)S(1)}, pred[8]{0:T(512)(128)(4,1)}, u32[]{:S(2)}) copy-start(pred[8]{0:T(512)(128)(4,1)} %copy-done.15) | copy-start | bytes 28
  196.0 5.4 %copy-start.18 = (s32[8]{0:T(128)S(1)}, s32[8]{0:T(128)}, u32[]{:S(2)}) copy-start(s32[8]{0:T(128)} %copy-done.17) | copy-start | bytes 100
  (12 other events, 15.1 us)

commit v2 on v0

v2 whole, which is shorter than its diff:
```python
import jax
import jax.numpy as jnp
from jax import lax
from jax.experimental import pallas as pl
from jax.experimental.pallas import tpu as pltpu
from jax.sharding import PartitionSpec as P

HEADS = 8


EPSILON = 1e-05


def row_stats(values):
    centred = values - jnp.mean(values, axis=-1, keepdims=True)
    scale = lax.rsqrt(jnp.mean(centred * centred, axis=-1, keepdims=True) + EPSILON)
    return centred * scale, scale


def norm_back(hat, scale, grad):
    drop = jnp.mean(grad, axis=-1, keepdims=True)
    slant = jnp.mean(grad * hat, axis=-1, keepdims=True)
    return scale * (grad - drop - hat * slant)


def dot(left, right, contract):
    return lax.dot_general(
        left, right, ((contract[:1], contract[1:]), ((), ())), preferred_element_type=jnp.float32
    )


def send_kernel(member_ref, index_ref, rows_ref, out_ref):
    own_count = rows_ref.shape[0]
    start = index_ref[0] * own_count
    for slot in range(own_count):
        member = member_ref[start + slot]

        @pl.when(member >= 0)
        def _():
            out_ref[jnp.maximum(member, 0)] = rows_ref[slot]


def send_rows(seq_member, index, own_rows, members):
    own_count, seq_span, model_width = own_rows.shape
    return pl.pallas_call(
        send_kernel,
        grid_spec=pltpu.PrefetchScalarGridSpec(
            num_scalar_prefetch=2,
            grid=(1,),
            in_specs=[pl.BlockSpec(own_rows.shape, lambda i, m, x: (0, 0, 0))],
            out_specs=pl.BlockSpec(
                (members, seq_span, model_width), lambda i, m, x: (0, 0, 0)
            ),
        ),
        out_shape=jax.ShapeDtypeStruct((members, seq_span, model_width), own_rows.dtype),
    )(seq_member, index, own_rows)


def take_kernel(member_ref, index_ref, back_ref, out_ref, sems):
    own_count = out_ref.shape[0]
    start = index_ref[0] * own_count

    def each(slot, act):
        member = member_ref[start + slot]

        @pl.when(member >= 0)
        def _():
            copy = pltpu.make_async_copy(
                back_ref.at[jnp.maximum(member, 0)], out_ref.at[slot], sems.at[slot]
            )
            act(copy)

        return member

    for slot in range(own_count):
        member = each(slot, lambda copy: copy.start())

        @pl.when(member < 0)
        def _():
            out_ref[slot] = jnp.zeros(out_ref.shape[1:], out_ref.dtype)

    for slot in range(own_count):
        each(slot, lambda copy: copy.wait())


def take_rows(seq_member, index, returned, own_count):
    _, seq_span, model_width = returned.shape
    return pl.pallas_call(
        take_kernel,
        grid_spec=pltpu.PrefetchScalarGridSpec(
            num_scalar_prefetch=2,
            grid=(1,),
            in_specs=[pl.BlockSpec(memory_space=pl.ANY)],
            out_specs=pl.BlockSpec((own_count, seq_span, model_width), lambda i, m, x: (0, 0, 0)),
            scratch_shapes=[pltpu.SemaphoreType.DMA((own_count,))],
        ),
        out_shape=jax.ShapeDtypeStruct((own_count, seq_span, model_width), returned.dtype),
    )(seq_member, index, returned)


def layer_kernel(
    source_ref, length_ref, core_ref,
    incoming_ref, cot_ref, wide_ref, narrow_ref,
    result_ref, back_ref, keep_ref, send_ref,
    x_ref, grad_ref, slope_ref, act_ref, score_ref, att_ref, proj_ref, term_ref, x_sems, out_sems,
):
    work, span, width = cot_ref.shape
    total = work * span
    head_size = width // HEADS
    pair = 2 * head_size
    pairs = HEADS // 2
    f32, bf16 = jnp.float32, jnp.bfloat16
    for p in range(work):
        pltpu.make_async_copy(incoming_ref.at[source_ref[p]], x_ref.at[p], x_sems.at[p]).start()

    row = lax.broadcasted_iota(jnp.int32, (total, 1), 0)
    seq, place = row // span, row % span
    length = jnp.full((total, 1), length_ref[0], jnp.int32)
    for p in range(1, work):
        length = jnp.where(seq == p, length_ref[p], length)
    live = place < length
    inverse = 1.0 / length.astype(f32)
    wide_row = lax.broadcasted_iota(jnp.int32, (total, total), 0)
    wide_col = lax.broadcasted_iota(jnp.int32, (total, total), 1)
    visible = (wide_row // span == wide_col // span) & (wide_col <= wide_row)
    causal = jnp.where(visible, inverse, 0.0)
    low_half = lax.broadcasted_iota(jnp.int32, (total, pair), 1) < head_size

    grad_live = jnp.where(live, cot_ref[...].reshape(total, width).astype(f32), 0.0).astype(bf16)
    grad_mixed = dot(grad_live, narrow_ref[...], (1, 1))

    for p in range(work):
        pltpu.make_async_copy(incoming_ref.at[source_ref[p]], x_ref.at[p], x_sems.at[p]).wait()
    rows = x_ref[...].reshape(total, width).astype(f32)
    hat, scale = row_stats(rows)
    normed = hat.astype(bf16)

    for part in range(4):
        cols = slice(part * width, (part + 1) * width)
        projected = dot(normed, wide_ref[:, cols], (1, 0))
        sigma = jax.nn.sigmoid(projected)
        act_ref[:, cols] = (projected * sigma).astype(bf16)
        slope_ref[:, cols] = sigma * (1.0 + projected * (1.0 - sigma))

    def half(values, which):
        return jnp.where(low_half if which == 0 else ~low_half, values, jnp.zeros_like(values))

    def block(part, g):
        return act_ref[:, part * width + g * pair : part * width + (g + 1) * pair]

    for g in range(pairs):
        value, query, key = block(1, g), block(2, g), block(3, g)
        attended = None
        for which in range(2):
            head = 2 * g + which
            scores = dot(half(query, which), key, (1, 1)) * head_size**-0.5
            score_ref[head] = scores
            weights = (scores * jax.nn.sigmoid(scores) * causal).astype(bf16)
            mixed_in = dot(weights, half(value, which), (1, 0))
            attended = mixed_in if attended is None else attended + mixed_in
        att_ref[:, g * pair : (g + 1) * pair] = attended

    att_hat, att_scale = row_stats(att_ref[...])
    gate = act_ref[:, :width].astype(f32)
    mixed = (att_hat * gate).astype(bf16)
    result = jnp.where(live, dot(mixed, narrow_ref[...], (1, 0)) + rows, 0.0)
    result_ref[...] = result.astype(bf16).reshape(work, span, width)

    def put_terms(values, col, size):
        term_ref[:, :, :, col : col + size] = values.astype(bf16).reshape(
            term_ref.shape[:3] + (size,)
        )

    put_terms(dot(mixed, grad_live, (0, 0)), 4 * width, width)

    grad_act = (grad_mixed * att_hat).astype(bf16).astype(f32)
    proj_ref[:, :width] = (grad_act * slope_ref[:, :width]).astype(bf16)
    grad_att = norm_back(att_hat, att_scale, grad_mixed * gate).astype(bf16)

    for g in range(pairs):
        value, query, key = block(1, g), block(2, g), block(3, g)
        grad_out = grad_att[:, g * pair : (g + 1) * pair]
        sums = [None, None, None]
        for which in range(2):
            head = 2 * g + which
            scores = score_ref[head]
            sigma = jax.nn.sigmoid(scores)
            weights = (scores * sigma * causal).astype(bf16)
            grad_half = half(grad_out, which)
            grad_weights = dot(grad_half, value, (1, 1))
            grad_scores = (
                grad_weights * causal * (sigma * (1.0 + scores * (1.0 - sigma))) * head_size**-0.5
            ).astype(bf16)
            grads = (
                dot(weights, grad_half, (0, 0)),
                dot(grad_scores, half(key, which), (1, 0)),
                dot(grad_scores, half(query, which), (0, 0)),
            )
            sums = [b if a is None else a + b for a, b in zip(sums, grads)]
        for part, grad in enumerate(sums):
            cols = slice((part + 1) * width + g * pair, (part + 1) * width + (g + 1) * pair)
            grad = grad.astype(bf16).astype(f32)
            proj_ref[:, cols] = (grad * slope_ref[:, cols]).astype(bf16)

    for part in range(4):
        cols = slice(part * width, (part + 1) * width)
        put_terms(dot(normed, proj_ref[:, cols], (0, 0)), part * width, width)
    core = core_ref[0]
    copies = [
        pltpu.make_async_copy(term_ref.at[:, core], keep_ref, out_sems.at[0]),
        pltpu.make_async_copy(term_ref.at[:, 1 - core], send_ref, out_sems.at[1]),
    ]
    for copy in copies:
        copy.start()

    grad_normed = dot(proj_ref[...], wide_ref[...], (1, 1))
    grad_rows = norm_back(hat, scale, grad_normed) + grad_live.astype(f32)
    grad_rows = jnp.where(live, grad_rows, 0.0).astype(bf16)
    grad_ref[...] = grad_rows.reshape(work, span, width)
    for p in range(work):
        copies.append(
            pltpu.make_async_copy(grad_ref.at[p], back_ref.at[source_ref[p]], out_sems.at[2 + p])
        )
        copies[-1].start()
    for copy in copies:
        copy.wait()


def run_layer(source, lengths, core, incoming, cotangent, w_uvqk, w_out):
    work, span, width = cotangent.shape
    members = incoming.shape[0]
    total, wide = work * span, w_uvqk.shape[1]
    part_rows, chips = width // members, members // 2
    whole = pl.BlockSpec(memory_space=pltpu.VMEM)
    far = pl.BlockSpec(memory_space=pl.ANY)
    bf16, f32 = jnp.bfloat16, jnp.float32
    half_terms = jax.ShapeDtypeStruct((chips, part_rows, wide + width), bf16)
    return pl.pallas_call(
        layer_kernel,
        grid_spec=pltpu.PrefetchScalarGridSpec(
            num_scalar_prefetch=3,
            grid=(1,),
            in_specs=[far, whole, whole, whole],
            out_specs=[whole, far, far, far],
            scratch_shapes=[
                pltpu.VMEM((work, span, width), bf16),
                pltpu.VMEM((work, span, width), bf16),
                pltpu.VMEM((total, wide), f32),
                pltpu.VMEM((total, wide), bf16),
                pltpu.VMEM((HEADS, total, total), f32),
                pltpu.VMEM((total, width), f32),
                pltpu.VMEM((total, wide), bf16),
                pltpu.VMEM((chips, 2, part_rows, wide + width), bf16),
                pltpu.SemaphoreType.DMA((work,)),
                pltpu.SemaphoreType.DMA((2 + work,)),
            ],
        ),
        out_shape=[
            jax.ShapeDtypeStruct(cotangent.shape, bf16),
            jax.ShapeDtypeStruct(incoming.shape, bf16),
            half_terms,
            half_terms,
        ],
    )(source, lengths, core, incoming, cotangent, w_uvqk, w_out)


def swap_pieces(pieces, axis, groups=None):
    return lax.all_to_all(
        pieces, axis, split_axis=0, concat_axis=0, tiled=True, axis_index_groups=groups
    )


def sum_pieces(pieces):
    return jnp.sum(pieces.astype(jnp.float32), axis=0).astype(jnp.bfloat16)


def reduce_terms(keep, send, model_width):
    members = lax.axis_size("bal")
    groups = lax.axis_size("grp")
    chips, part_rows, width = keep.shape
    same_core = [[2 * chip + core for chip in range(chips)] for core in range(2)]
    received = lax.ppermute(send, "bal", [(m, m ^ 1) for m in range(members)])
    chip_sum = (keep.astype(jnp.float32) + received.astype(jnp.float32)).astype(jnp.bfloat16)
    part = sum_pieces(swap_pieces(chip_sum, "bal", same_core))
    near, far = 4, groups // 4
    near_groups = [[near * block + i for i in range(near)] for block in range(far)]
    far_groups = [[near * block + i for block in range(far)] for i in range(near)]
    pieces = part.reshape(part_rows, near, width // near).transpose(1, 0, 2)
    piece = sum_pieces(swap_pieces(pieces, "grp", near_groups))
    copies = jnp.broadcast_to(piece[None], (far,) + piece.shape)
    piece = sum_pieces(swap_pieces(copies, "grp", far_groups))
    copies = jnp.broadcast_to(piece[None], (near,) + piece.shape)
    total = swap_pieces(copies, "grp", near_groups)
    total = total.transpose(1, 0, 2).reshape(part_rows, width).astype(jnp.float32)
    return total[:, : width - model_width], total[:, width - model_width :]


def work_sources(seq_lengths, seq_member, my_index, own_count, work_count):
    members = seq_member.shape[0] // own_count
    to_me = (seq_member.reshape(members, own_count) == my_index).astype(jnp.int32)
    owns = jnp.sum(to_me, axis=1)
    item_length = jnp.sum(to_me * seq_lengths.reshape(members, own_count), axis=1)
    ids = jnp.arange(members)
    position = jnp.sum(jnp.where(ids[None, :] < ids[:, None], owns[None, :], 0), axis=1)
    picked = (owns[None, :] > 0) & (position[None, :] == jnp.arange(work_count)[:, None])
    picked = picked.astype(jnp.int32)
    source = jnp.sum(picked * ids[None, :].astype(jnp.int32), axis=1)
    return source, jnp.sum(picked * item_length[None, :], axis=1)


def body(own_rows, work_cotangent, seq_lengths, seq_member, w_uvqk, w_out):
    members = lax.axis_size("bal")
    my_index = lax.axis_index("bal").astype(jnp.int32)
    own_count, _, model_width = own_rows.shape
    work_count = work_cotangent.shape[0]
    index = my_index[None]
    incoming = swap_pieces(send_rows(seq_member, index, own_rows, members), "bal")
    source, lengths = work_sources(seq_lengths, seq_member, my_index, own_count, work_count)
    result, back, keep, send = run_layer(
        source, lengths, index % 2, incoming, work_cotangent, w_uvqk, w_out
    )
    own_grad = take_rows(seq_member, index, swap_pieces(back, "bal"), own_count)
    grad_uvqk, grad_out = reduce_terms(keep, send, model_width)
    return (result, own_grad, grad_uvqk, grad_out)


def solution(mesh):
    placed = (
        P(("grp", "bal"), None, None),
        P(("grp", "bal"), None, None),
        P("grp"),
        P("grp"),
        P(),
        P(),
    )
    return jax.shard_map(
        body,
        mesh=mesh,
        in_specs=placed,
        out_specs=(
            P(("grp", "bal"), None, None),
            P(("grp", "bal"), None, None),
            P("bal", None),
            P("bal", None),
        ),
        check_vma=False,
    )
```

time: 610 us -> 168 us (0.28)
  the two profiles are of different devices: /device:TPU:2 before, /device:TPU:1 now
where the time goes in v2:
time: 168 us; the launch traced here: 167 us
  blocking collectives  75.1 us (45%)
  waiting for transfers between devices  38.1 us (23%)
  starting transfers between devices  33 us (20%)
  Pallas kernels  14.1 us (8%)
  local copies, waits for them, and re-layouts  3.18 us (2%)
  other arithmetic  3.01 us (2%)
    all_to_all x3, blocking collectives, swap_pieces(): lax.all_to_all(pieces, axis, split_axis=0, concat_axis=0, tiled=True, axi...  75.1 us
    all_to_all x3, waiting for transfers between devices, swap_pieces(): lax.all_to_all(pieces, axis, split_axis=0, concat_axis=0, tiled=True, axi...  35 us
    all_to_all x3, starting transfers between devices, swap_pieces(): lax.all_to_all(pieces, axis, split_axis=0, concat_axis=0, tiled=True, axi...  31 us
    pallas_call x1, Pallas kernels, run_layer(): pl.pallas_call(layer_kernel, grid_spec=pltpu.PrefetchScalarGridSpec(num_s...  9.05 us
  transfers between devices with their start and end apart: 4, of which 4 were waited for; matrix products, arithmetic and copies ran while one was open for 1% of the time, Pallas kernels for 1%

profile of v2, /device:TPU:1, one launch (start us, length us, event | category | flops | bytes accessed | tf_op | source)
XLA Modules:
  0.0 167.3 jit_solution(17161190888348792313)
XLA Ops:
  0.6 2.7 %shard_map.93 = bf16[32,32,512]{2,1,0:T(8,128)(2,1)} custom-call(s32[256]{0:T(256)} %member_ref.3, s32[1]{0:T(128)} %bitcast.index_ref, bf16[8,32,512]{2,1,0:T(8,128)(2,1)} %rows_ref.1), custom_call_target="tpu_custom_call" | custom-call | tf_op jit(solution)/shard_map/pallas_call | solution.py:45
  3.3 17.8 %all-to-all-start = ((bf16[32,32,512]{2,1,0:T(8,128)(2,1)}), bf16[32,32,512]{2,1,0:T(8,128)(2,1)S(1)}, u32[]{:S(2)}, u32[]{:S(2)}) async-start(bf16[32,32,512]{2,1,0:T(8,128)(2,1)} %shard_map.93), calls=%async_computation | async-start | bytes 2097152 | tf_op jit(solution)/shard_map/all_to_all | solution.py:268
  21.3 0.1 reduce_sum.81
  21.4 0.1 reduce_sum.84
  21.6 0.1 select_reduce_fusion
  21.7 0.7 select_reduce_fusion.1
  22.4 15.8 %all-to-all-done.incoming_ref = bf16[32,32,512]{2,1,0:T(8,128)(2,1)S(1)} async-done(((bf16[32,32,512]{2,1,0:T(8,128)(2,1)}), bf16[32,32,512]{2,1,0:T(8,128)(2,1)S(1)}, u32[]{:S(2)}, u32[]{:S(2)}) %all-to-all-start) | async-done | bytes 1048608 | tf_op jit(solution)/shard_map/all_to_all | solution.py:268
  38.1 1.0 copy-done
  39.1 9.1 %shard_map.94 = (bf16[4,32,512]{2,1,0:T(8,128)(2,1)}, bf16[32,32,512]{2,1,0:T(8,128)(2,1)}, bf16[16,16,2560]{2,1,0:T(8,128)(2,1)}, bf16[16,16,2560]{2,1,0:T(8,128)(2,1)}) custom-call(s32[4]{0:T(128)} %get-tuple-element.13.source_ref, s32[4]{0:T(128)} %get-tuple-element.12.length_ref, s32[1]{0:T(128)S(6)} %select_n.12.core_ref, bf16[32,32,512]{2,1,0:T(8,128)(2,1)} %copy-done, ...), custom_call_target="tpu_custom_call" | custom-call | tf_op jit(solution)/shard_map/pallas_call | solution.py:238
  48.2 2.0 %collective-permute-start = (bf16[16,16,2560]{2,1,0:T(8,128)(2,1)}, bf16[16,16,2560]{2,1,0:T(8,128)(2,1)S(1)}, u32[]{:S(2)}, u32[]{:S(2)}) collective-permute-start(bf16[16,16,2560]{2,1,0:T(8,128)(2,1)} %get-tuple-element.11), channel_id=1, source_target_pairs={{0,1},{1,0},{2,3},{3,2},{4,5},{5,4},{6,7},{7,6},{8,9},{9,8},{10,11... | collective-permute-start | bytes 3932168 | tf_op jit(solution)/shard_map/ppermute | solution.py:282
  50.2 3.1 %collective-permute-done = bf16[16,16,2560]{2,1,0:T(8,128)(2,1)S(1)} collective-permute-done((bf16[16,16,2560]{2,1,0:T(8,128)(2,1)}, bf16[16,16,2560]{2,1,0:T(8,128)(2,1)S(1)}, u32[]{:S(2)}, u32[]{:S(2)}) %collective-permute-start) | collective-permute-done | bytes 1310752 | tf_op jit(solution)/shard_map/ppermute | solution.py:282
  53.3 1.8 %add_convert_fusion = bf16[16,16,2560]{2,1,0:T(8,128)(2,1)S(1)} fusion(bf16[16,16,2560]{2,1,0:T(8,128)(2,1)S(1)} %collective-permute-done, bf16[16,16,2560]{2,1,0:T(8,128)(2,1)} %get-tuple-element.10), kind=kLoop, calls=%fused_computation | loop fusion | flops 2621440 | bytes 3932160 | tf_op jit(solution)/shard_map/convert_element_type | solution.py:283
  55.1 21.9 %all_to_all.30 = bf16[16,16,2560]{2,1,0:T(8,128)(2,1)S(1)} all-to-all(bf16[16,16,2560]{2,1,0:T(8,128)(2,1)S(1)} %add_convert_fusion), channel_id=1, replica_groups={{0,2,4,6,8,10,12,14,16,18,20,22,24,26,28,30},{1,3,5,7,9,11,13,15,17,19,..., dimensions={0} | all-to-all | bytes 2621440 | tf_op jit(solution)/shard_map/all_to_all | solution.py:268
  77.0 0.2 reduce_sum.86
  77.2 7.0 %all_to_all.31 = bf16[4,16,640]{2,1,0:T(8,128)(2,1)S(1)} all-to-all(bf16[4,16,640]{2,1,0:T(8,128)(2,1)S(1)} %copy.12), channel_id=1, replica_groups={{0,32,64,96},{128,160,192,224},{256,288,320,352},{384,416,448,480},{512..., dimensions={0} | all-to-all | bytes 163840 | tf_op jit(solution)/shard_map/all_to_all | solution.py:268
  84.2 46.2 %all_to_all.32 = bf16[8,16,640]{2,1,0:T(8,128)(2,1)S(1)} all-to-all(bf16[8,16,640]{2,1,0:T(8,128)(2,1)S(1)} %broadcast_in_dim.21), channel_id=1, replica_groups={{0,128,256,384,512,640,768,896},{32,160,288,416,544,672,800,928},{64,19..., dimensions={0} | all-to-all | bytes 327680 | tf_op jit(solution)/shard_map/all_to_all | solution.py:268
  130.4 10.0 %all-to-all-start.1 = ((bf16[32,32,512]{2,1,0:T(8,128)(2,1)}), bf16[32,32,512]{2,1,0:T(8,128)(2,1)S(1)}, u32[]{:S(2)}, u32[]{:S(2)}) async-start(bf16[32,32,512]{2,1,0:T(8,128)(2,1)} %get-tuple-element.9), calls=%async_computation.1 | async-start | bytes 2097152 | tf_op jit(solution)/shard_map/all_to_all | solution.py:268
  140.4 16.9 %all-to-all-done.1.back_ref = bf16[32,32,512]{2,1,0:T(8,128)(2,1)S(1)} async-done(((bf16[32,32,512]{2,1,0:T(8,128)(2,1)}), bf16[32,32,512]{2,1,0:T(8,128)(2,1)S(1)}, u32[]{:S(2)}, u32[]{:S(2)}) %all-to-all-start.1) | async-done | bytes 1048608 | tf_op jit(solution)/shard_map/all_to_all | solution.py:268
  157.3 0.7 broadcast_in_dim.22
  158.0 3.3 %all-to-all-start.5 = ((bf16[4,16,640]{2,1,0:T(8,128)(2,1)}), bf16[4,16,640]{2,1,0:T(8,128)(2,1)S(1)}, u32[]{:S(2)}, u32[]{:S(2)}) async-start(bf16[4,16,640]{2,1,0:T(8,128)(2,1)} %broadcast_in_dim.22), calls=%async_computation.5 | async-start | bytes 163840 | tf_op jit(solution)/shard_map/all_to_all | solution.py:268
  161.3 2.3 %shard_map.95 = bf16[8,32,512]{2,1,0:T(8,128)(2,1)} custom-call(s32[256]{0:T(256)} %member_ref.3, s32[1]{0:T(128)} %bitcast.index_ref, bf16[32,32,512]{2,1,0:T(8,128)(2,1)} %copy-done.1), custom_call_target="tpu_custom_call" | custom-call | tf_op jit(solution)/shard_map/pallas_call | solution.py:88
  163.7 2.3 %all-to-all-done.5 = bf16[4,16,640]{2,1,0:T(8,128)(2,1)S(1)} async-done(((bf16[4,16,640]{2,1,0:T(8,128)(2,1)}), bf16[4,16,640]{2,1,0:T(8,128)(2,1)S(1)}, u32[]{:S(2)}, u32[]{:S(2)}) %all-to-all-start.5) | async-done | bytes 81952 | tf_op jit(solution)/shard_map/all_to_all | solution.py:268
  166.0 0.6 slice.9
  166.7 0.7 slice.8
  (19 shorter events, 0.3 us)
Async XLA Ops:
  3.3 17.8 %copy-start.2 = (s32[256]{0:T(256)S(1)}, s32[256]{0:T(256)}, u32[]{:S(2)}) copy-start(s32[256]{0:T(256)} %member_ref.3) | copy-start | bytes 3076
  3.3 17.9 %copy-start.3 = (s32[256]{0:T(256)S(1)}, s32[256]{0:T(256)}, u32[]{:S(2)}) copy-start(s32[256]{0:T(256)} %param.8) | copy-start | bytes 3076
  3.3 34.8 %all-to-all-start = ((bf16[32,32,512]{2,1,0:T(8,128)(2,1)}), bf16[32,32,512]{2,1,0:T(8,128)(2,1)S(1)}, u32[]{:S(2)}, u32[]{:S(2)}) async-start(bf16[32,32,512]{2,1,0:T(8,128)(2,1)} %shard_map.93), calls=%async_computation | async-start | bytes 2097152 | tf_op jit(solution)/shard_map/all_to_all | solution.py:268
  38.1 1.0 copy-start
  48.2 5.1 %collective-permute-start = (bf16[16,16,2560]{2,1,0:T(8,128)(2,1)}, bf16[16,16,2560]{2,1,0:T(8,128)(2,1)S(1)}, u32[]{:S(2)}, u32[]{:S(2)}) collective-permute-start(bf16[16,16,2560]{2,1,0:T(8,128)(2,1)} %get-tuple-element.11), channel_id=1, source_target_pairs={{0,1},{1,0},{2,3},{3,2},{4,5},{5,4},{6,7},{7,6},{8,9},{9,8},{10,11... | collective-permute-start | bytes 3932168 | tf_op jit(solution)/shard_map/ppermute | solution.py:282
  130.4 26.9 %all-to-all-start.1 = ((bf16[32,32,512]{2,1,0:T(8,128)(2,1)}), bf16[32,32,512]{2,1,0:T(8,128)(2,1)S(1)}, u32[]{:S(2)}, u32[]{:S(2)}) async-start(bf16[32,32,512]{2,1,0:T(8,128)(2,1)} %get-tuple-element.9), calls=%async_computation.1 | async-start | bytes 2097152 | tf_op jit(solution)/shard_map/all_to_all | solution.py:268
  157.3 4.0 %copy-start.1 = (bf16[32,32,512]{2,1,0:T(8,128)(2,1)}, bf16[32,32,512]{2,1,0:T(8,128)(2,1)S(1)}, u32[]{:S(2)}) copy-start(bf16[32,32,512]{2,1,0:T(8,128)(2,1)S(1)} %all-to-all-done.1.back_ref) | copy-start | bytes 3145732
  158.0 8.0 %all-to-all-start.5 = ((bf16[4,16,640]{2,1,0:T(8,128)(2,1)}), bf16[4,16,640]{2,1,0:T(8,128)(2,1)S(1)}, u32[]{:S(2)}, u32[]{:S(2)}) async-start(bf16[4,16,640]{2,1,0:T(8,128)(2,1)} %broadcast_in_dim.22), calls=%async_computation.5 | async-start | bytes 163840 | tf_op jit(solution)/shard_map/all_to_all | solution.py:268

commit v3 on v2

v3 whole, which is shorter than its diff:
```python
import jax
import jax.numpy as jnp
from jax import lax
from jax.experimental import pallas as pl
from jax.experimental.pallas import tpu as pltpu
from jax.sharding import PartitionSpec as P

HEADS = 8


EPSILON = 1e-05


def row_stats(values):
    centred = values - jnp.mean(values, axis=-1, keepdims=True)
    scale = lax.rsqrt(jnp.mean(centred * centred, axis=-1, keepdims=True) + EPSILON)
    return centred * scale, scale


def norm_back(hat, scale, grad):
    drop = jnp.mean(grad, axis=-1, keepdims=True)
    slant = jnp.mean(grad * hat, axis=-1, keepdims=True)
    return scale * (grad - drop - hat * slant)


def dot(left, right, contract):
    return lax.dot_general(
        left, right, ((contract[:1], contract[1:]), ((), ())), preferred_element_type=jnp.float32
    )


def send_kernel(member_ref, index_ref, cot_ref, out_ref):
    members = out_ref.shape[0]
    own_count = member_ref.shape[0] // members
    work_count = cot_ref.shape[0]
    mine = index_ref[0]

    def each(owner, place):
        found = member_ref[owner * own_count] == mine
        for slot in range(1, own_count):
            found = found | (member_ref[owner * own_count + slot] == mine)

        @pl.when(found)
        def _():
            out_ref[owner] = cot_ref[jnp.minimum(place, work_count - 1)]

        return place + found.astype(jnp.int32)

    lax.fori_loop(0, members, each, jnp.int32(0))


def send_cotangent(seq_member, index, cotangent, members):
    _, seq_span, model_width = cotangent.shape
    return pl.pallas_call(
        send_kernel,
        grid_spec=pltpu.PrefetchScalarGridSpec(
            num_scalar_prefetch=2,
            grid=(1,),
            in_specs=[pl.BlockSpec(cotangent.shape, lambda i, m, x: (0, 0, 0))],
            out_specs=pl.BlockSpec(
                (members, seq_span, model_width), lambda i, m, x: (0, 0, 0)
            ),
        ),
        out_shape=jax.ShapeDtypeStruct((members, seq_span, model_width), cotangent.dtype),
    )(seq_member, index, cotangent)


def take_kernel(source_ref, back_ref, out_ref):
    for place in range(out_ref.shape[0]):
        out_ref[place] = back_ref[source_ref[place]]


def take_result(source, returned, work_count):
    _, seq_span, model_width = returned.shape
    whole = pl.BlockSpec(memory_space=pltpu.VMEM)
    return pl.pallas_call(
        take_kernel,
        grid_spec=pltpu.PrefetchScalarGridSpec(
            num_scalar_prefetch=1, grid=(1,), in_specs=[whole], out_specs=whole
        ),
        out_shape=jax.ShapeDtypeStruct((work_count, seq_span, model_width), returned.dtype),
    )(source, returned)


def row_lengths(length_ref, start, own_count, span):
    seq = lax.broadcasted_iota(jnp.int32, (own_count * span, 1), 0) // span
    place = lax.broadcasted_iota(jnp.int32, (own_count * span, 1), 0) % span
    length = jnp.full((own_count * span, 1), length_ref[start], jnp.int32)
    for slot in range(1, own_count):
        length = jnp.where(seq == slot, length_ref[start + slot], length)
    return length, place < length


def forward_kernel(
    member_ref, length_ref, index_ref,
    rows_ref, wide_ref, narrow_ref,
    slots_ref, act_ref, slope_ref, weight_ref, bend_ref, att_ref, mixed_ref,
    result_ref, sems,
):
    own_count, span, width = rows_ref.shape
    total = own_count * span
    square = weight_ref.shape[-1]
    head_size = width // HEADS
    pair = 2 * head_size
    f32, bf16 = jnp.float32, jnp.bfloat16
    start = index_ref[0] * own_count
    length, live = row_lengths(length_ref, start, own_count, span)
    inverse = jnp.where(length > 0, 1.0 / jnp.maximum(length, 1).astype(f32), 0.0)
    wide_row = lax.broadcasted_iota(jnp.int32, (square, square), 0)
    wide_col = lax.broadcasted_iota(jnp.int32, (square, square), 1)
    visible = (wide_row // span == wide_col // span) & (wide_col <= wide_row)
    low_half = lax.broadcasted_iota(jnp.int32, (square, pair), 1) < head_size

    rows = rows_ref[...].reshape(total, width).astype(f32)
    normed = row_stats(rows)[0].astype(bf16)
    for part in range(4):
        cols = slice(part * width, (part + 1) * width)
        projected = dot(normed, wide_ref[:, cols], (1, 0))
        sigma = jax.nn.sigmoid(projected)
        act_ref[:, cols] = (projected * sigma).astype(bf16)
        slope_ref[:, cols] = (sigma * (1.0 + projected * (1.0 - sigma))).astype(bf16)

    for cut in range(total // square):
        span_rows = slice(cut * square, (cut + 1) * square)
        causal = jnp.where(visible, inverse[span_rows], 0.0)
        for g in range(HEADS // 2):
            value, query, key = (
                act_ref[span_rows, part * width + g * pair : part * width + (g + 1) * pair]
                for part in (1, 2, 3)
            )
            attended = None
            for which in range(2):
                keep = low_half if which == 0 else ~low_half
                scores = dot(jnp.where(keep, query, 0), key, (1, 1)) * head_size**-0.5
                sigma = jax.nn.sigmoid(scores)
                weights = (scores * sigma * causal).astype(bf16)
                weight_ref[cut, 2 * g + which] = weights
                bend = sigma * (1.0 + scores * (1.0 - sigma)) * causal * head_size**-0.5
                bend_ref[cut, 2 * g + which] = bend.astype(bf16)
                part_sum = dot(weights, jnp.where(keep, value, 0), (1, 0))
                attended = part_sum if attended is None else attended + part_sum
            att_ref[span_rows, g * pair : (g + 1) * pair] = attended

    att_hat, _ = row_stats(att_ref[...])
    mixed = (att_hat * act_ref[:, :width].astype(f32)).astype(bf16)
    mixed_ref[...] = mixed
    result = jnp.where(live, dot(mixed, narrow_ref[...], (1, 0)) + rows, 0.0)
    result_ref[...] = result.astype(bf16).reshape(own_count, span, width)

    for act in ("start", "wait"):
        for slot in range(own_count):
            member = member_ref[start + slot]

            @pl.when(member >= 0)
            def _():
                copy = pltpu.make_async_copy(
                    result_ref.at[slot], slots_ref.at[jnp.maximum(member, 0)], sems.at[slot]
                )
                getattr(copy, act)()


def run_forward(seq_member, seq_lengths, index, own_rows, w_uvqk, w_out, members):
    own_count, span, width = own_rows.shape
    total, wide = own_count * span, w_uvqk.shape[1]
    square = min(128, total)
    whole = pl.BlockSpec(memory_space=pltpu.VMEM)
    far = pl.BlockSpec(memory_space=pl.ANY)
    bf16, f32 = jnp.bfloat16, jnp.float32
    squares = jax.ShapeDtypeStruct((total // square, HEADS, square, square), bf16)
    return pl.pallas_call(
        forward_kernel,
        grid_spec=pltpu.PrefetchScalarGridSpec(
            num_scalar_prefetch=3,
            grid=(1,),
            in_specs=[whole, whole, whole],
            out_specs=[far] + [whole] * 6,
            scratch_shapes=[
                pltpu.VMEM((own_count, span, width), bf16),
                pltpu.SemaphoreType.DMA((own_count,)),
            ],
        ),
        out_shape=[
            jax.ShapeDtypeStruct((members, span, width), bf16),
            jax.ShapeDtypeStruct((total, wide), bf16),
            jax.ShapeDtypeStruct((total, wide), bf16),
            squares,
            squares,
            jax.ShapeDtypeStruct((total, width), f32),
            jax.ShapeDtypeStruct((total, width), bf16),
        ],
    )(seq_member, seq_lengths, index, own_rows, w_uvqk, w_out)


def backward_kernel(
    member_ref, length_ref, index_ref,
    incoming_ref, rows_ref, wide_ref, narrow_ref,
    act_ref, slope_ref, weight_ref, bend_ref, att_ref, mixed_ref,
    grad_ref, keep_ref, send_ref,
    cot_ref, proj_ref, term_ref, out_sems,
):
    own_count, span, width = rows_ref.shape
    total = own_count * span
    square = weight_ref.shape[-1]
    head_size = width // HEADS
    pair = 2 * head_size
    f32, bf16 = jnp.float32, jnp.bfloat16
    start = index_ref[0] * own_count
    _, live = row_lengths(length_ref, start, own_count, span)
    low_half = lax.broadcasted_iota(jnp.int32, (square, pair), 1) < head_size

    for slot in range(own_count):
        cot_ref[slot] = incoming_ref[jnp.maximum(member_ref[start + slot], 0)]
    cot = cot_ref[...].reshape(total, width).astype(f32)
    grad_live = jnp.where(live, cot, 0.0).astype(bf16)
    grad_mixed = dot(grad_live, narrow_ref[...], (1, 1))

    def put_terms(values, col, size):
        term_ref[:, :, :, col : col + size] = values.astype(bf16).reshape(
            term_ref.shape[:3] + (size,)
        )

    put_terms(dot(mixed_ref[...], grad_live, (0, 0)), 4 * width, width)

    att_hat, att_scale = row_stats(att_ref[...])
    gate = act_ref[:, :width].astype(f32)
    grad_act = (grad_mixed * att_hat).astype(bf16).astype(f32)
    proj_ref[:, :width] = (grad_act * slope_ref[:, :width].astype(f32)).astype(bf16)
    grad_att = norm_back(att_hat, att_scale, grad_mixed * gate).astype(bf16)

    for cut in range(total // square):
        span_rows = slice(cut * square, (cut + 1) * square)
        for g in range(HEADS // 2):
            value, query, key = (
                act_ref[span_rows, part * width + g * pair : part * width + (g + 1) * pair]
                for part in (1, 2, 3)
            )
            grad_out = grad_att[span_rows, g * pair : (g + 1) * pair]
            sums = [None, None, None]
            for which in range(2):
                keep = low_half if which == 0 else ~low_half
                grad_half = jnp.where(keep, grad_out, 0)
                grad_weights = dot(grad_half, value, (1, 1))
                bend = bend_ref[cut, 2 * g + which].astype(f32)
                grad_scores = (grad_weights * bend).astype(bf16)
                grads = (
                    dot(weight_ref[cut, 2 * g + which], grad_half, (0, 0)),
                    dot(grad_scores, jnp.where(keep, key, 0), (1, 0)),
                    dot(grad_scores, jnp.where(keep, query, 0), (0, 0)),
                )
                sums = [b if a is None else a + b for a, b in zip(sums, grads)]
            for part, grad in enumerate(sums):
                cols = slice((part + 1) * width + g * pair, (part + 1) * width + (g + 1) * pair)
                grad = grad.astype(bf16).astype(f32)
                proj_ref[span_rows, cols] = (
                    grad * slope_ref[span_rows, cols].astype(f32)
                ).astype(bf16)

    rows = rows_ref[...].reshape(total, width).astype(f32)
    hat, scale = row_stats(rows)
    normed = hat.astype(bf16)
    for part in range(4):
        cols = slice(part * width, (part + 1) * width)
        put_terms(dot(normed, proj_ref[:, cols], (0, 0)), part * width, width)
    core = lax.rem(index_ref[0], 2)
    copies = [
        pltpu.make_async_copy(term_ref.at[:, core], keep_ref, out_sems.at[0]),
        pltpu.make_async_copy(term_ref.at[:, 1 - core], send_ref, out_sems.at[1]),
    ]
    for copy in copies:
        copy.start()

    grad_normed = dot(proj_ref[...], wide_ref[...], (1, 1))
    grad_rows = norm_back(hat, scale, grad_normed) + grad_live.astype(f32)
    grad_rows = jnp.where(live, grad_rows, 0.0).astype(bf16)
    grad_ref[...] = grad_rows.reshape(own_count, span, width)
    for copy in copies:
        copy.wait()


def run_backward(seq_member, seq_lengths, index, incoming, own_rows, w_uvqk, w_out, saved):
    own_count, span, width = own_rows.shape
    members = incoming.shape[0]
    total, wide = own_count * span, w_uvqk.shape[1]
    part_rows, chips = width // members, members // 2
    whole = pl.BlockSpec(memory_space=pltpu.VMEM)
    far = pl.BlockSpec(memory_space=pl.ANY)
    bf16 = jnp.bfloat16
    half_terms = jax.ShapeDtypeStruct((chips, part_rows, wide + width), bf16)
    return pl.pallas_call(
        backward_kernel,
        grid_spec=pltpu.PrefetchScalarGridSpec(
            num_scalar_prefetch=3,
            grid=(1,),
            in_specs=[whole] * (4 + len(saved)),
            out_specs=[whole, far, far],
            scratch_shapes=[
                pltpu.VMEM((own_count, span, width), bf16),
                pltpu.VMEM((total, wide), bf16),
                pltpu.VMEM((chips, 2, part_rows, wide + width), bf16),
                pltpu.SemaphoreType.DMA((2,)),
            ],
        ),
        out_shape=[
            jax.ShapeDtypeStruct(own_rows.shape, bf16),
            half_terms,
            half_terms,
        ],
    )(seq_member, seq_lengths, index, incoming, own_rows, w_uvqk, w_out, *saved)


def swap_pieces(pieces, axis, groups=None):
    return lax.all_to_all(
        pieces, axis, split_axis=0, concat_axis=0, tiled=True, axis_index_groups=groups
    )


def sum_pieces(pieces):
    return jnp.sum(pieces.astype(jnp.float32), axis=0).astype(jnp.bfloat16)


def sum_pair(keep, send):
    members = lax.axis_size("bal")
    received = lax.ppermute(send, "bal", [(m, m ^ 1) for m in range(members)])
    return (keep.astype(jnp.float32) + received.astype(jnp.float32)).astype(jnp.bfloat16)


def reduce_terms(chip_sum, model_width):
    groups = lax.axis_size("grp")
    chips, part_rows, width = chip_sum.shape
    near, far = 4, groups // 4
    same_core = [[2 * chip + core for chip in range(chips)] for core in range(2)]
    near_groups = [[near * block + i for i in range(near)] for block in range(far)]
    far_groups = [[near * block + i for block in range(far)] for i in range(near)]
    part = sum_pieces(swap_pieces(chip_sum, "bal", same_core))
    pieces = part.reshape(part_rows, near, width // near).transpose(1, 0, 2)
    piece = sum_pieces(swap_pieces(pieces, "grp", near_groups))
    copies = jnp.broadcast_to(piece[None], (far,) + piece.shape)
    piece = sum_pieces(swap_pieces(copies, "grp", far_groups))
    copies = jnp.broadcast_to(piece[None], (near,) + piece.shape)
    total = swap_pieces(copies, "grp", near_groups)
    total = total.transpose(1, 0, 2).reshape(part_rows, width).astype(jnp.float32)
    return total[:, : width - model_width], total[:, width - model_width :]


def work_sources(seq_member, my_index, own_count, work_count):
    members = seq_member.shape[0] // own_count
    to_me = (seq_member.reshape(members, own_count) == my_index).astype(jnp.int32)
    owns = jnp.sum(to_me, axis=1)
    ids = jnp.arange(members)
    position = jnp.sum(jnp.where(ids[None, :] < ids[:, None], owns[None, :], 0), axis=1)
    picked = (owns[None, :] > 0) & (position[None, :] == jnp.arange(work_count)[:, None])
    return jnp.sum(picked.astype(jnp.int32) * ids[None, :].astype(jnp.int32), axis=1)


def body(own_rows, work_cotangent, seq_lengths, seq_member, w_uvqk, w_out):
    members = lax.axis_size("bal")
    my_index = lax.axis_index("bal").astype(jnp.int32)
    own_count, _, model_width = own_rows.shape
    work_count = work_cotangent.shape[0]
    index = my_index[None]
    outgoing = send_cotangent(seq_member, index, work_cotangent, members)
    incoming = swap_pieces(outgoing, "bal")
    slots, *saved = run_forward(seq_member, seq_lengths, index, own_rows, w_uvqk, w_out, members)
    returned = swap_pieces(slots, "bal")
    own_grad, keep, send = run_backward(
        seq_member, seq_lengths, index, incoming, own_rows, w_uvqk, w_out, saved
    )
    chip_sum = sum_pair(keep, send)
    returned, chip_sum = lax.optimization_barrier((returned, chip_sum))
    grad_uvqk, grad_out = reduce_terms(chip_sum, model_width)
    source = work_sources(seq_member, my_index, own_count, work_count)
    return (take_result(source, returned, work_count), own_grad, grad_uvqk, grad_out)


def solution(mesh):
    placed = (
        P(("grp", "bal"), None, None),
        P(("grp", "bal"), None, None),
        P("grp"),
        P("grp"),
        P(),
        P(),
    )
    return jax.shard_map(
        body,
        mesh=mesh,
        in_specs=placed,
        out_specs=(
            P(("grp", "bal"), None, None),
            P(("grp", "bal"), None, None),
            P("bal", None),
            P("bal", None),
        ),
        check_vma=False,
    )
```

time: 168 us -> 163 us (0.970)
  the two profiles are of different devices: /device:TPU:1 before, /device:TPU:8 now
where the time goes in v3:
time: 163 us; the launch traced here: 162 us
  blocking collectives  80.7 us (50%)
  starting transfers between devices  28.2 us (17%)
  Pallas kernels  23.1 us (14%)
  waiting for transfers between devices  22.5 us (14%)
  local copies, waits for them, and re-layouts  4.14 us (3%)
  other arithmetic  2.84 us (2%)
    all_to_all x3, blocking collectives, swap_pieces(): lax.all_to_all(pieces, axis, split_axis=0, concat_axis=0, tiled=True, axi...  80.7 us
    all_to_all x3, starting transfers between devices, swap_pieces(): lax.all_to_all(pieces, axis, split_axis=0, concat_axis=0, tiled=True, axi...  26.2 us
    all_to_all x3, waiting for transfers between devices, swap_pieces(): lax.all_to_all(pieces, axis, split_axis=0, concat_axis=0, tiled=True, axi...  22.5 us
    pallas_call x1, Pallas kernels, run_backward(): pl.pallas_call(backward_kernel, grid_spec=pltpu.PrefetchScalarGridSpec(nu...  9.72 us
    pallas_call x1, Pallas kernels, run_forward(): pl.pallas_call(forward_kernel, grid_spec=pltpu.PrefetchScalarGridSpec(num...  8.23 us
  transfers between devices with their start and end apart: 4, of which 3 were waited for; matrix products, arithmetic and copies ran while one was open for 2% of the time, Pallas kernels for 7%

profile of v3, /device:TPU:8, one launch (start us, length us, event | category | flops | bytes accessed | tf_op | source)
XLA Modules:
  0.0 162.3 jit_solution(8427338470045008473)
XLA Ops:
  0.6 2.6 %shard_map.94 = bf16[32,32,512]{2,1,0:T(8,128)(2,1)} custom-call(s32[256]{0:T(256)} %member_ref.5, s32[1]{0:T(128)} %bitcast.index_ref, bf16[4,32,512]{2,1,0:T(8,128)(2,1)} %cot_ref.1), custom_call_target="tpu_custom_call" | custom-call | tf_op jit(solution)/shard_map/pallas_call | solution.py:54
  3.3 16.8 %all-to-all-start.1 = ((bf16[32,32,512]{2,1,0:T(8,128)(2,1)}), bf16[32,32,512]{2,1,0:T(8,128)(2,1)S(1)}, u32[]{:S(2)}, u32[]{:S(2)}) async-start(bf16[32,32,512]{2,1,0:T(8,128)(2,1)} %shard_map.94), calls=%async_computation.1 | async-start | bytes 2097152 | tf_op jit(solution)/shard_map/all_to_all | solution.py:312
  20.0 8.2 %shard_map.93 = (bf16[32,32,512]{2,1,0:T(8,128)(2,1)}, bf16[256,2048]{1,0:T(8,128)(2,1)}, bf16[256,2048]{1,0:T(8,128)(2,1)}, bf16[2,8,128,128]{3,2,1,0:T(8,128)(...) custom-call(s32[256]{0:T(256)} %member_ref.5, s32[256]{0:T(256)} %length_ref.3, ...), custom_call_target="tpu_custom_call" | custom-call | tf_op jit(solution)/shard_map/pallas_call | solution.py:170
  28.3 7.4 %all-to-all-done.1.incoming_ref = bf16[32,32,512]{2,1,0:T(8,128)(2,1)S(1)} async-done(((bf16[32,32,512]{2,1,0:T(8,128)(2,1)}), bf16[32,32,512]{2,1,0:T(8,128)(2,1)S(1)}, u32[]{:S(2)}, u32[]{:S(2)}) %all-to-all-start.1) | async-done | bytes 1048608 | tf_op jit(solution)/shard_map/all_to_all | solution.py:312
  35.7 1.0 copy-done
  36.7 9.7 %shard_map.95 = (bf16[8,32,512]{2,1,0:T(8,128)(2,1)}, bf16[16,16,2560]{2,1,0:T(8,128)(2,1)}, bf16[16,16,2560]{2,1,0:T(8,128)(2,1)}) custom-call(s32[256]{0:T(256)} %member_ref.5, s32[256]{0:T(256)} %length_ref.3, s32[1]{0:T(128)} %bitcast.index_ref, bf16[32,32,512]{2,1,0:T(8,128)(2,1)} %copy-done, bf16[8,32,512]{2,1,0:T(8,128)(2,1)} %rows_ref.3, ...), custom_call_target="tpu_custom_call" | custom-call | tf_op jit(solution)/shard_map/pallas_call | solution.py:289
  46.4 2.1 %collective-permute-start = (bf16[16,16,2560]{2,1,0:T(8,128)(2,1)}, bf16[16,16,2560]{2,1,0:T(8,128)(2,1)S(1)}, u32[]{:S(2)}, u32[]{:S(2)}) collective-permute-start(bf16[16,16,2560]{2,1,0:T(8,128)(2,1)} %get-tuple-element.24), channel_id=1, source_target_pairs={{0,1},{1,0},{2,3},{3,2},{4,5},{5,4},{6,7},{7,6},{8,9},{9,8},{10,11... | collective-permute-start | bytes 3932168 | tf_op jit(solution)/shard_map/ppermute | solution.py:323
  48.5 6.1 %all-to-all-start = ((bf16[32,32,512]{2,1,0:T(8,128)(2,1)}), bf16[32,32,512]{2,1,0:T(8,128)(2,1)}, u32[]{:S(2)}, u32[]{:S(2)}) async-start(bf16[32,32,512]{2,1,0:T(8,128)(2,1)} %get-tuple-element.16), calls=%async_computation | async-start | bytes 2097152 | tf_op jit(solution)/shard_map/all_to_all | solution.py:312
  54.6 1.1 copy-done.2
  55.7 1.7 %add_convert_fusion = bf16[16,16,2560]{2,1,0:T(8,128)(2,1)S(1)} fusion(bf16[16,16,2560]{2,1,0:T(8,128)(2,1)} %copy-done.2, bf16[16,16,2560]{2,1,0:T(8,128)(2,1)S(1)} %copy-done.1), kind=kLoop, calls=%fused_computation | loop fusion | flops 2621440 | bytes 3932160 | tf_op jit(solution)/shard_map/convert_element_type | solution.py:324
  57.4 12.8 %all-to-all-done.back_ref = bf16[32,32,512]{2,1,0:T(8,128)(2,1)} async-done(((bf16[32,32,512]{2,1,0:T(8,128)(2,1)}), bf16[32,32,512]{2,1,0:T(8,128)(2,1)}, u32[]{:S(2)}, u32[]{:S(2)}) %all-to-all-start) | async-done | bytes 1048608 | tf_op jit(solution)/shard_map/all_to_all | solution.py:312
  70.3 23.3 %all_to_all.30 = bf16[16,16,2560]{2,1,0:T(8,128)(2,1)S(1)} all-to-all(bf16[16,16,2560]{2,1,0:T(8,128)(2,1)S(1)} %add_convert_fusion), channel_id=1, replica_groups={{0,2,4,6,8,10,12,14,16,18,20,22,24,26,28,30},{1,3,5,7,9,11,13,15,17,19,..., dimensions={0} | all-to-all | bytes 2621440 | tf_op jit(solution)/shard_map/all_to_all | solution.py:312
  93.6 0.2 reduce_sum.66
  93.9 8.2 %all_to_all.31 = bf16[4,16,640]{2,1,0:T(8,128)(2,1)S(1)} all-to-all(bf16[4,16,640]{2,1,0:T(8,128)(2,1)S(1)} %copy.12), channel_id=1, replica_groups={{0,32,64,96},{128,160,192,224},{256,288,320,352},{384,416,448,480},{512..., dimensions={0} | all-to-all | bytes 163840 | tf_op jit(solution)/shard_map/all_to_all | solution.py:312
  102.1 49.2 %all_to_all.32 = bf16[8,16,640]{2,1,0:T(8,128)(2,1)S(1)} all-to-all(bf16[8,16,640]{2,1,0:T(8,128)(2,1)S(1)} %broadcast_in_dim.21), channel_id=1, replica_groups={{0,128,256,384,512,640,768,896},{32,160,288,416,544,672,800,928},{64,19..., dimensions={0} | all-to-all | bytes 327680 | tf_op jit(solution)/shard_map/all_to_all | solution.py:312
  151.3 0.6 broadcast_in_dim.22
  152.0 3.3 %all-to-all-start.5 = ((bf16[4,16,640]{2,1,0:T(8,128)(2,1)}), bf16[4,16,640]{2,1,0:T(8,128)(2,1)S(1)}, u32[]{:S(2)}, u32[]{:S(2)}) async-start(bf16[4,16,640]{2,1,0:T(8,128)(2,1)} %broadcast_in_dim.22), calls=%async_computation.5 | async-start | bytes 163840 | tf_op jit(solution)/shard_map/all_to_all | solution.py:312
  155.4 0.1 reduce_sum.63
  155.5 0.1 select_reduce_fusion
  155.6 0.6 select_reduce_fusion.1.source_ref
  156.3 2.5 %shard_map.96 = bf16[4,32,512]{2,1,0:T(8,128)(2,1)} custom-call(s32[4]{0:T(128)} %select_reduce_fusion.1.source_ref, bf16[32,32,512]{2,1,0:T(8,128)(2,1)} %all-to-all-done.back_ref), custom_call_target="tpu_custom_call" | custom-call | tf_op jit(solution)/shard_map/pallas_call | solution.py:76
  158.8 2.2 %all-to-all-done.5 = bf16[4,16,640]{2,1,0:T(8,128)(2,1)S(1)} async-done(((bf16[4,16,640]{2,1,0:T(8,128)(2,1)}), bf16[4,16,640]{2,1,0:T(8,128)(2,1)S(1)}, u32[]{:S(2)}, u32[]{:S(2)}) %all-to-all-start.5) | async-done | bytes 81952 | tf_op jit(solution)/shard_map/all_to_all | solution.py:312
  161.1 0.7 slice.8
  161.7 0.6 slice.9
  (17 shorter events, 0.2 us)
Async XLA Ops:
  3.3 32.4 %all-to-all-start.1 = ((bf16[32,32,512]{2,1,0:T(8,128)(2,1)}), bf16[32,32,512]{2,1,0:T(8,128)(2,1)S(1)}, u32[]{:S(2)}, u32[]{:S(2)}) async-start(bf16[32,32,512]{2,1,0:T(8,128)(2,1)} %shard_map.94), calls=%async_computation.1 | async-start | bytes 2097152 | tf_op jit(solution)/shard_map/all_to_all | solution.py:312
  35.7 1.0 copy-start
  46.4 9.3 %copy-start.1 = (bf16[16,16,2560]{2,1,0:T(8,128)(2,1)S(1)}, bf16[16,16,2560]{2,1,0:T(8,128)(2,1)}, u32[]{:S(2)}) copy-start(bf16[16,16,2560]{2,1,0:T(8,128)(2,1)} %get-tuple-element.23) | copy-start | bytes 3932164
  46.4 8.2 %collective-permute-start = (bf16[16,16,2560]{2,1,0:T(8,128)(2,1)}, bf16[16,16,2560]{2,1,0:T(8,128)(2,1)S(1)}, u32[]{:S(2)}, u32[]{:S(2)}) collective-permute-start(bf16[16,16,2560]{2,1,0:T(8,128)(2,1)} %get-tuple-element.24), channel_id=1, source_target_pairs={{0,1},{1,0},{2,3},{3,2},{4,5},{5,4},{6,7},{7,6},{8,9},{9,8},{10,11... | collective-permute-start | bytes 3932168 | tf_op jit(solution)/shard_map/ppermute | solution.py:323
  48.5 21.8 %all-to-all-start = ((bf16[32,32,512]{2,1,0:T(8,128)(2,1)}), bf16[32,32,512]{2,1,0:T(8,128)(2,1)}, u32[]{:S(2)}, u32[]{:S(2)}) async-start(bf16[32,32,512]{2,1,0:T(8,128)(2,1)} %get-tuple-element.16), calls=%async_computation | async-start | bytes 2097152 | tf_op jit(solution)/shard_map/all_to_all | solution.py:312
  54.6 1.1 copy-start.2
  93.6 61.7 %copy-start.3 = (s32[256]{0:T(256)S(1)}, s32[256]{0:T(256)}, u32[]{:S(2)}) copy-start(s32[256]{0:T(256)} %member_ref.5) | copy-start | bytes 3076
  152.0 9.1 %all-to-all-start.5 = ((bf16[4,16,640]{2,1,0:T(8,128)(2,1)}), bf16[4,16,640]{2,1,0:T(8,128)(2,1)S(1)}, u32[]{:S(2)}, u32[]{:S(2)}) async-start(bf16[4,16,640]{2,1,0:T(8,128)(2,1)} %broadcast_in_dim.22), calls=%async_computation.5 | async-start | bytes 163840 | tf_op jit(solution)/shard_map/all_to_all | solution.py:312
